TPU v7x, 32 devices: a whole 2x2x4 slice. The times are simulated.
32 devices in a mesh: gx: 16 (over z, y, x), gy: 2 (over core).
Axes of the slice: x: 2, y: 2, z: 4, core: 2. Of those that a mesh axis runs over, the one named last changes fastest.
Arguments:
- displacement: float32 [3, 32, 128, 256], P(None, None, 'gx', 'gy'), may hold values from -6 to 6
- velocity: float32 [3, 32, 128, 256], P(None, None, 'gx', 'gy'), may hold values from -6 to 6
- slopes: float32 [2, 32, 128, 256], P(None, None, 'gx', 'gy'), may hold values from -0.5 to 0.5
- stretch: float32 [32, 128, 256], P(None, 'gx', 'gy'), may hold values from 0.6 to 1.4
- moduli: float32 [2, 32, 128, 256], P(None, None, 'gx', 'gy'), may hold values from 0.3 to 1
- buoyancy: float32 [32, 128, 256], P(None, 'gx', 'gy'), may hold values from 0.5 to 1.5
- probes: float32 [4, 128, 128], P(None, 'gy'), may hold values from -0.0048828125 to 0.0048828125
Outputs:
- final_displacement: float32 [3, 32, 128, 256], P(None, None, 'gx', 'gy')
- basis: float32 [64, 48, 128], P('gx', 'gy')
- factor: float32 [128, 128], replicated
All inputs are finite; a program needn't handle non-finite values.
Results may differ from a plain program's by a relative error of at most 0.0003.
Values sent between devices are 32-bit elements; how exact they have to be, the bound alone decides.
No kernel may reach another device: no remote copies, remote signals or barrier semaphores. Data moves between devices by JAX's collectives and lax.ppermute only.
A program may use at most 64 MiB of HBM per device.

v0:
```python
import math
import jax
import jax.numpy as jnp
from jax import lax
from jax.sharding import PartitionSpec as P

STEPS = 4
time_step = 0.12


def extended(block, sides, width):
    for axis, dim in sides:
        count = lax.axis_size(axis)
        forward = [(i, i + 1) for i in range(count - 1)]
        backward = [(target, source) for source, target in forward]
        low = lax.ppermute(
            lax.slice_in_dim(block, block.shape[dim] - width, None, axis=dim), axis, forward
        )
        high = lax.ppermute(lax.slice_in_dim(block, 0, width, axis=dim), axis, backward)
        block = jnp.concatenate([low, block, high], axis=dim)
    return block


def fourth(values, dimension):
    length_out = values.shape[dimension] - 4

    def segment(offset):
        return lax.slice_in_dim(values, offset, offset + length_out, axis=dimension)

    return (segment(0) - segment(4) + 8.0 * (segment(3) - segment(1))) / 12.0


def vertical(values):
    padded = jnp.pad(values, ((0, 0), (2, 2), (0, 0), (0, 0)))
    return fourth(padded, 1)


def gradient(padded, slope_x, slope_y, stretch):
    d_x = fourth(padded[:, :, :, 2:-2], 2)
    d_y = fourth(padded[:, :, 2:-2, :], 3)
    d_r = vertical(padded[:, :, 2:-2, 2:-2])
    return jnp.stack([d_x + slope_x * d_r, d_y + slope_y * d_r, stretch * d_r], axis=1)


def stresses(gradients, lame, shear):
    divergence = gradients[0, 0] + gradients[1, 1] + gradients[2, 2]
    pressure = lame * divergence
    return jnp.stack(
        [
            pressure + 2.0 * shear * gradients[0, 0],
            pressure + 2.0 * shear * gradients[1, 1],
            pressure + 2.0 * shear * gradients[2, 2],
            shear * (gradients[0, 1] + gradients[1, 0]),
            shear * (gradients[0, 2] + gradients[2, 0]),
            shear * (gradients[1, 2] + gradients[2, 1]),
        ]
    )


def forces(padded, slope_x, slope_y, stretch):
    d_x = fourth(padded[:, :, :, 2:-2], 2)
    d_y = fourth(padded[:, :, 2:-2, :], 3)
    d_r = vertical(padded[:, :, 2:-2, 2:-2])
    rows_x = (0, 3, 4)
    rows_y = (3, 1, 5)
    rows_z = (4, 5, 2)
    return jnp.stack(
        [
            d_x[rows_x[component]]
            + slope_x * d_r[rows_x[component]]
            + d_y[rows_y[component]]
            + slope_y * d_r[rows_y[component]]
            + stretch * d_r[rows_z[component]]
            for component in range(3)
        ]
    )


def lower_factor(gram):
    order = gram.shape[0]
    positions = jnp.arange(order, dtype=jnp.int32)

    def column_step(column_index, lower):
        picker = (positions == column_index).astype(jnp.float32)
        column = jnp.dot(gram, picker, precision=lax.Precision.HIGHEST)
        row_of = jnp.dot(picker, lower, precision=lax.Precision.HIGHEST)
        column = column - jnp.dot(lower, row_of, precision=lax.Precision.HIGHEST)
        pivot = jnp.sqrt(jnp.sum(column * picker))
        entries = jnp.where(
            positions > column_index,
            column / pivot,
            jnp.where(positions == column_index, pivot, 0.0),
        )
        return lower + entries[:, None] * picker[None, :]

    return lax.fori_loop(0, order, column_step, jnp.zeros_like(gram))


def lower_inverse(lower):
    order = lower.shape[0]
    positions = jnp.arange(order, dtype=jnp.int32)

    def row_step(row_index, inverse):
        picker = (positions == row_index).astype(jnp.float32)
        row_of = jnp.dot(picker, lower, precision=lax.Precision.HIGHEST)
        pivot = jnp.sum(row_of * picker)
        fresh = (picker - jnp.dot(row_of, inverse, precision=lax.Precision.HIGHEST)) / pivot
        return inverse + picker[:, None] * fresh[None, :]

    return lax.fori_loop(0, order, row_step, jnp.zeros_like(lower))


def orthogonalize(tall_block, gram):
    lower = lower_factor(gram)
    inverse = lower_inverse(lower)
    result = jnp.dot(
        tall_block, inverse.T, precision=lax.Precision.HIGHEST, preferred_element_type=jnp.float32
    )
    return (result, lower.T)


def shards(displacement, velocity, slopes, stretch, moduli, buoyancy, probes):
    previous = displacement - time_step * velocity
    current = displacement
    stacked = jnp.concatenate([slopes, stretch[None], moduli], 0)
    near_values = extended(stacked, (("gx", 2), ("gy", 3)), 2)
    for moment in range(STEPS):
        padded = extended(current, (("gx", 2), ("gy", 3)), 4)
        gradients = gradient(padded, near_values[0], near_values[1], near_values[2])
        stress = stresses(gradients, near_values[3], near_values[4])
        pushes = buoyancy * forces(stress, slopes[0], slopes[1], stretch)
        following = 2.0 * current - previous + time_step**2 * pushes
        velocities = (following - previous) / (2.0 * time_step)
        sampled = velocities[:, ::2, ::2, ::2]
        half_x = sampled.shape[2]
        rearranged = jnp.transpose(sampled, (2, 0, 1, 3)).reshape(-1, sampled.shape[3])
        sketch_term = jnp.dot(
            rearranged,
            probes[moment],
            precision=lax.Precision.HIGHEST,
            preferred_element_type=jnp.float32,
        ).reshape(half_x, -1, probes.shape[2])
        reduced = lax.psum_scatter(sketch_term, "gy", scatter_dimension=1, tiled=True)
        sketch = reduced if moment == 0 else sketch + reduced
        previous, current = (current, following)
    tall_block = sketch.reshape(-1, sketch.shape[2])
    rows_total = tall_block.shape[0] * lax.axis_size("gx") * lax.axis_size("gy")
    gram_local = jnp.dot(
        tall_block.T,
        tall_block,
        precision=lax.Precision.HIGHEST,
        preferred_element_type=jnp.float32,
    )
    gram_whole = lax.psum(gram_local, ("gx", "gy"))
    orthonormal, factor = orthogonalize(tall_block, gram_whole)
    basis = (math.sqrt(rows_total) * orthonormal).reshape(sketch.shape)
    return (current, basis, factor)


def solution(mesh):
    in_specs = (
        P(None, None, "gx", "gy"),
        P(None, None, "gx", "gy"),
        P(None, None, "gx", "gy"),
        P(None, "gx", "gy"),
        P(None, None, "gx", "gy"),
        P(None, "gx", "gy"),
        P(None, "gy", None),
    )
    out_specs = (P(None, None, "gx", "gy"), P("gx", "gy", None), P())
    return jax.shard_map(shards, mesh=mesh, in_specs=in_specs, out_specs=out_specs, check_vma=False)
```

profile of v0, /device:TPU:1, one launch (start us, length us, event | category | flops | bytes accessed | tf_op | source)
XLA Modules:
  0.0 987.9 jit_solution(11689234760993657389)
XLA Ops:
  10.5 5.2 collective-permute-start
  18.5 4.9 collective-permute-start.4
  31.3 4.7 collective-permute-start.3
  44.7 4.6 pad_maximum_fusion
  63.1 3.5 fusion.87
  67.4 4.9 fusion.56
  72.4 3.3 add_multiply_fusion.3
  79.5 3.9 collective-permute-start.8
  86.8 5.7 collective-permute-done.9
  92.8 3.6 collective-permute-start.11
  104.1 3.5 fusion.78
  108.5 4.5 fusion.50
  113.0 3.3 add_multiply_fusion.2
  123.0 6.1 collective-permute-start.12
  132.6 6.9 slice.1053
  146.8 3.0 collective-permute-start.15
  152.7 6.9 slice.1055
  165.3 2.9 fusion.74
  168.3 3.5 fusion.69
  172.6 4.9 fusion.44
  177.6 3.3 add_multiply_fusion.1
  191.6 5.8 collective-permute-start.16
  199.1 6.9 slice.1057
  212.1 3.9 collective-permute-start.19
  223.9 3.5 fusion.60
  228.2 4.9 fusion.38
  233.2 3.3 add_multiply_fusion
  241.1 7.0 slice.1059
  250.0 7.7 reduce-scatter.2.cloned.1.call-done
  260.7 125.2 %all-reduce.10.cloned.1.call-done = f32[128,128]{1,0:T(8,128)} async-done(((f32[128,128]{1,0:T(8,128)}), f32[128,128]{1,0:T(8,128)}) %all-reduce.10.cloned.1.call-update) | async-done | bytes 65552 | tf_op jit(solution)/shard_map/psum | solution.py:154
  385.8 363.3 %while.30 = (s32[]{:T(128)}, f32[128,128]{1,0:T(8,128)S(1)}, f32[128,128]{1,0:T(8,128)}, s32[]{:T(128)}, s32[]{:T(128)}) while((s32[]{:T(128)}, f32[128,128]{1,0:T(8,128)S(1)}, f32[128,128]{1,0:T(8,128)}, s32[]{:T(128)}, s32[]{:T(128)}) %tuple.121), condition=%wide.region_7.8_spmd.clone.clone, body=%wide.region_5.7_spmd.clone.clone.sunk | while | flops 673410 | bytes 332917 | solution.py:96
  749.9 230.0 %while.29 = (s32[]{:T(128)}, f32[128,128]{1,0:T(8,128)S(1)}, f32[128,128]{1,0:T(8,128)S(1)}, s32[]{:T(128)}, s32[]{:T(128)}) while((s32[]{:T(128)}, f32[128,128]{1,0:T(8,128)S(1)}, f32[128,128]{1,0:T(8,128)S(1)}, s32[]{:T(128)}, s32[]{:T(128)}) %tuple.124), condition=%wide.region_10.11_spmd.clone, body=%wide.region_8.10_spmd.clone.sunk | while | flops 460034 | bytes 265316 | solution.py:110
  (1549 shorter events, 612.5 us)
Async XLA Ops:
  7.2 250.4 %reduce-scatter.2.cloned.1.call-start = ((), (), s32[]{:S(2)}) async-start(), calls=%async_computation.2 | async-start | bytes 147456 | tf_op jit(solution)/shard_map/reduce_scatter | solution.py:143
  9.2 17.0 %collective-permute-start.1 = (f32[5,32,2,128]{3,1,2,0:T(8,128)}, f32[5,32,2,128]{3,1,2,0:T(8,128)}, u32[]{:S(2)}, u32[]{:S(2)}) collective-permute-start(f32[5,32,2,128]{3,1,2,0:T(8,128)} %copy.382), channel_id=1, source_target_pairs={{2,0},{4,2},{6,4},{8,6},{10,8},{12,10},{14,12},{16,14},{18,16},{20... | collective-permute-start | bytes 491528 | tf_op jit(solution)/shard_map/ppermute | solution.py:19
  10.5 14.3 %collective-permute-start = (f32[5,32,2,128]{3,1,2,0:T(8,128)S(1)}, f32[5,32,2,128]{3,1,2,0:T(8,128)}, u32[]{:S(2)}, u32[]{:S(2)}) collective-permute-start(f32[5,32,2,128]{3,1,2,0:T(8,128)S(1)} %copy.381), channel_id=1, source_target_pairs={{0,2},{2,4},{4,6},{6,8},{8,10},{10,12},{12,14},{14,16},{16,18},{18... | collective-permute-start | bytes 491528 | tf_op jit(solution)/shard_map/ppermute | solution.py:16
  16.5 34.9 %collective-permute-start.5 = (f32[3,32,4,128]{3,1,2,0:T(8,128)}, f32[3,32,4,128]{3,1,2,0:T(8,128)}, u32[]{:S(2)}, u32[]{:S(2)}) collective-permute-start(f32[3,32,4,128]{3,1,2,0:T(8,128)} %copy.384), channel_id=1, source_target_pairs={{2,0},{4,2},{6,4},{8,6},{10,8},{12,10},{14,12},{16,14},{18,16},{20... | collective-permute-start | bytes 589832 | tf_op jit(solution)/shard_map/ppermute | solution.py:19
  18.5 30.8 %collective-permute-start.4 = (f32[3,32,4,128]{3,1,2,0:T(8,128)}, f32[3,32,4,128]{3,1,2,0:T(8,128)}, u32[]{:S(2)}, u32[]{:S(2)}) collective-permute-start(f32[3,32,4,128]{3,1,2,0:T(8,128)} %copy.383), channel_id=1, source_target_pairs={{0,2},{2,4},{4,6},{6,8},{8,10},{10,12},{12,14},{14,16},{16,18},{18... | collective-permute-start | bytes 589832 | tf_op jit(solution)/shard_map/ppermute | solution.py:16
  26.2 10.5 %copy-start.50 = (f32[5,32,2,128]{1,3,2,0:T(8,128)}, f32[5,32,2,128]{1,3,2,0:T(8,128)S(1)}, u32[]{:S(2)}) copy-start(f32[5,32,2,128]{1,3,2,0:T(8,128)S(1)} %copy.315) | copy-start | bytes 491524
  30.0 14.7 %collective-permute-start.2 = (f32[5,32,12,2]{1,3,2,0:T(2,128)}, f32[5,32,12,2]{1,3,2,0:T(2,128)}, u32[]{:S(2)}, u32[]{:S(2)}) collective-permute-start(f32[5,32,12,2]{1,3,2,0:T(2,128)} %get-tuple-element.285), channel_id=1, source_target_pairs={{0,1},{2,3},{4,5},{6,7},{8,9},{10,11},{12,13},{14,15},{16,17},{18,... | collective-permute-start | bytes 46088 | tf_op jit(solution)/shard_map/ppermute | solution.py:16
  31.3 13.4 %collective-permute-start.3 = (f32[5,32,12,2]{1,3,2,0:T(2,128)}, f32[5,32,12,2]{1,3,2,0:T(2,128)}, u32[]{:S(2)}, u32[]{:S(2)}) collective-permute-start(f32[5,32,12,2]{1,3,2,0:T(2,128)} %get-tuple-element.286), channel_id=1, source_target_pairs={{1,0},{3,2},{5,4},{7,6},{9,8},{11,10},{13,12},{15,14},{17,16},{19,... | collective-permute-start | bytes 46088 | tf_op jit(solution)/shard_map/ppermute | solution.py:19
  37.8 37.8 %copy-start.25 = (f32[32,8,128]{0,2,1:T(8,128)}, f32[32,8,128]{0,2,1:T(8,128)S(1)}, u32[]{:S(2)}) copy-start(f32[32,8,128]{0,2,1:T(8,128)S(1)} %copy.331) | copy-start | bytes 393220
  39.5 37.1 %copy-start.6 = (f32[3,32,8,128]{1,3,2,0:T(8,128)}, f32[3,32,8,128]{1,3,2,0:T(8,128)S(1)}, u32[]{:S(2)}) copy-start(f32[3,32,8,128]{1,3,2,0:T(8,128)S(1)} %copy.309) | copy-start | bytes 1179652
  39.7 35.9 %copy-start.29 = (f32[1,32,8,128]{1,3,2,0:T(8,128)}, f32[1,32,8,128]{1,3,2,0:T(8,128)S(1)}, u32[]{:S(2)}) copy-start(f32[1,32,8,128]{1,3,2,0:T(8,128)S(1)} %copy.385) | copy-start | bytes 393220
  40.0 35.7 %copy-start.33 = (f32[1,32,8,128]{1,3,2,0:T(8,128)}, f32[1,32,8,128]{1,3,2,0:T(8,128)S(1)}, u32[]{:S(2)}) copy-start(f32[1,32,8,128]{1,3,2,0:T(8,128)S(1)} %copy.386) | copy-start | bytes 393220
  54.5 4.8 collective-permute-start.7
  55.9 3.4 collective-permute-start.6
  79.5 7.0 collective-permute-start.8
  83.6 8.8 collective-permute-start.9
  92.8 4.9 collective-permute-start.11
  96.4 3.2 collective-permute-start.10
  123.0 17.4 %collective-permute-start.12 = (f32[3,32,4,128]{3,1,2,0:T(8,128)}, f32[3,32,4,128]{3,1,2,0:T(8,128)}, u32[]{:S(2)}, u32[]{:S(2)}) collective-permute-start(f32[3,32,4,128]{3,1,2,0:T(8,128)} %copy.348), channel_id=1, source_target_pairs={{0,2},{2,4},{4,6},{6,8},{8,10},{10,12},{12,14},{14,16},{16,18},{18... | collective-permute-start | bytes 589832 | tf_op jit(solution)/shard_map/ppermute | solution.py:16
  131.1 11.3 %collective-permute-start.13 = (f32[3,32,4,128]{3,1,2,0:T(8,128)}, f32[3,32,4,128]{3,1,2,0:T(8,128)}, u32[]{:S(2)}, u32[]{:S(2)}) collective-permute-start(f32[3,32,4,128]{3,1,2,0:T(8,128)} %copy.349), channel_id=1, source_target_pairs={{2,0},{4,2},{6,4},{8,6},{10,8},{12,10},{14,12},{16,14},{18,16},{20... | collective-permute-start | bytes 589832 | tf_op jit(solution)/shard_map/ppermute | solution.py:19
  146.8 13.6 %collective-permute-start.15 = (f32[3,32,16,4]{1,2,3,0:T(8,128)}, f32[3,32,16,4]{1,2,3,0:T(8,128)}, u32[]{:S(2)}, u32[]{:S(2)}) collective-permute-start(f32[3,32,16,4]{1,2,3,0:T(8,128)} %copy.353), channel_id=1, source_target_pairs={{1,0},{3,2},{5,4},{7,6},{9,8},{11,10},{13,12},{15,14},{17,16},{19,... | collective-permute-start | bytes 73736 | tf_op jit(solution)/shard_map/ppermute | solution.py:19
  149.8 11.6 %collective-permute-start.14 = (f32[3,32,16,4]{1,2,3,0:T(8,128)}, f32[3,32,16,4]{1,2,3,0:T(8,128)}, u32[]{:S(2)}, u32[]{:S(2)}) collective-permute-start(f32[3,32,16,4]{1,2,3,0:T(8,128)} %copy.352), channel_id=1, source_target_pairs={{0,1},{2,3},{4,5},{6,7},{8,9},{10,11},{12,13},{14,15},{16,17},{18,... | collective-permute-start | bytes 73736 | tf_op jit(solution)/shard_map/ppermute | solution.py:16
  186.2 11.2 %copy-start.56 = (f32[4,48,128]{2,1,0:T(8,128)S(1)}, f32[4,48,128]{2,1,0:T(8,128)}, u32[]{:S(2)}) copy-start(f32[4,48,128]{2,1,0:T(8,128)} %fusion.203) | copy-start | bytes 294916
  186.2 11.2 %copy-start.59 = (f32[4,3,16,64]{3,2,1,0:T(8,128)S(1)}, f32[4,3,16,64]{3,2,1,0:T(8,128)}, u32[]{:S(2)}) copy-start(f32[4,3,16,64]{3,2,1,0:T(8,128)} %copy.376) | copy-start | bytes 147460
  188.2 22.9 %copy-start.5 = (f32[3,32,8,128]{1,3,2,0:T(8,128)S(1)}, f32[3,32,8,128]{1,3,2,0:T(8,128)}, u32[]{:S(2)}) copy-start(f32[3,32,8,128]{1,3,2,0:T(8,128)} %copy-done.4) | copy-start | bytes 1179652
  190.3 18.6 %collective-permute-start.17 = (f32[3,32,4,128]{3,1,2,0:T(8,128)}, f32[3,32,4,128]{3,1,2,0:T(8,128)}, u32[]{:S(2)}, u32[]{:S(2)}) collective-permute-start(f32[3,32,4,128]{3,1,2,0:T(8,128)} %copy.362), channel_id=1, source_target_pairs={{2,0},{4,2},{6,4},{8,6},{10,8},{12,10},{14,12},{16,14},{18,16},{20... | collective-permute-start | bytes 589832 | tf_op jit(solution)/shard_map/ppermute | solution.py:19
  191.6 15.2 %collective-permute-start.16 = (f32[3,32,4,128]{3,1,2,0:T(8,128)}, f32[3,32,4,128]{3,1,2,0:T(8,128)}, u32[]{:S(2)}, u32[]{:S(2)}) collective-permute-start(f32[3,32,4,128]{3,1,2,0:T(8,128)} %copy.361), channel_id=1, source_target_pairs={{0,2},{2,4},{4,6},{6,8},{8,10},{10,12},{12,14},{14,16},{16,18},{18... | collective-permute-start | bytes 589832 | tf_op jit(solution)/shard_map/ppermute | solution.py:16
  212.1 6.3 collective-permute-start.19
  216.1 3.2 collective-permute-start.18
  241.0 18.4 %copy-start.49 = (f32[3,32,8,128]{1,3,2,0:T(8,128)S(1)}, f32[3,32,8,128]{1,3,2,0:T(8,128)}, u32[]{:S(2)}) copy-start(f32[3,32,8,128]{1,3,2,0:T(8,128)} %get-tuple-element.231) | copy-start | bytes 1179652
  249.9 135.9 %all-reduce.10.cloned.1.call-start = ((), (), s32[]{:S(2)}) async-start(), calls=%async_computation.1 | async-start | bytes 131072 | tf_op jit(solution)/shard_map/psum | solution.py:154
  259.5 720.5 %copy-start.55 = (f32[4,24,128]{2,1,0:T(8,128)S(1)}, f32[4,24,128]{2,1,0:T(8,128)}, u32[]{:S(2)}) copy-start(f32[4,24,128]{2,1,0:T(8,128)} %reduce-scatter.2.cloned.1.call-done) | copy-start | bytes 147460
  (51 other events, 188.8 us)
Sparse Core Ops, SparseCore 0:
  250.0 7.5 reduce-scatter.1
  263.8 122.0 all-reduce.9
where the time goes:
time: 1000 us; the launch traced here: 988 us
  matrix products  478 us (48%)
  waiting for transfers between devices  142 us (14%)
  other arithmetic  116 us (12%)
  loops' own time  98.3 us (10%)
  local copies, waits for them, and re-layouts  81.5 us (8%)
  starting transfers between devices  56.2 us (6%)
  between operations  15.7 us (2%)
    psum x1, waiting for transfers between devices, shards(): gram_whole = lax.psum(gram_local, ('gx', 'gy'))  125 us
    dot_general x128, matrix products, column_step(): column = jnp.dot(gram, picker, precision=lax.Precision.HIGHEST)  124 us
    dot_general x128, matrix products, column_step(): column = column - jnp.dot(lower, row_of, precision=lax.Precision.HIGHEST)  108 us
    dot_general x128, matrix products, row_step(): jnp.dot(row_of, inverse, precision=lax.Precision.HIGHEST)  107 us
    dot_general x128, matrix products, row_step(): row_of = jnp.dot(picker, lower, precision=lax.Precision.HIGHEST)  105 us
    another operation x1, loops' own time, lower_factor(): return lax.fori_loop(0, order, column_step, jnp.zeros_like(gram))  94 us
    ppermute x10, starting transfers between devices, extended(): lax.ppermute(lax.slice_in_dim(block, block.shape[dim] - width, None, axis...  32.5 us
    div x8, other arithmetic, fourth(): return (segment(0) - segment(4) + 8.0 * (segment(3) - segment(1))) / 12.0  32.5 us
  transfers between devices with their start and end apart: 22, of which 6 were waited for; matrix products, arithmetic and copies ran while one was open for 6% of the time, Pallas kernels for 0%

commit v1 on v0

--- a/solution.py
+++ b/solution.py
@@ -151,7 +151,8 @@
         precision=lax.Precision.HIGHEST,
         preferred_element_type=jnp.float32,
     )
-    gram_whole = lax.psum(gram_local, ("gx", "gy"))
+    blocks = lax.all_gather(gram_local, ("gx", "gy"), axis=0, tiled=False)
+    gram_whole = blocks.sum(axis=0)
     orthonormal, factor = orthogonalize(tall_block, gram_whole)
     basis = (math.sqrt(rows_total) * orthonormal).reshape(sketch.shape)
     return (current, basis, factor)

time: 1000 us -> 823 us (0.82)
  matrix products: 478 us -> 370 us
  waiting for transfers between devices: 142 us -> 75 us
    psum x1 -> x0, waiting for transfers between devices: 125 us -> none  [shards(): gram_whole = lax.psum(gram_local, ('gx', 'gy'))]
    dot_general x128, matrix products: 124 us -> 16.4 us  [column_step(): column = jnp.dot(gram, picker, precision=lax.Precision.HIGHEST)]
    all_gather x0 -> x1, waiting for transfers between devices: none -> 57.8 us  [shards(): blocks = lax.all_gather(gram_local, ('gx', 'gy'), axis=0, tiled=False)]
  transfers between devices with their start and end apart: 22 -> 22, of which waited for: 6 -> 6; matrix products, arithmetic and copies ran while one was open for 6% -> 8% of each run, Pallas kernels for 0% -> 0%
where the time goes in v1:
time: 823 us; the launch traced here: 815 us
  matrix products  370 us (45%)
  other arithmetic  118 us (14%)
  loops' own time  98.3 us (12%)
  local copies, waits for them, and re-layouts  81.5 us (10%)
  waiting for transfers between devices  75 us (9%)
  starting transfers between devices  56.2 us (7%)
  between operations  15.7 us (2%)
    dot_general x128, matrix products, column_step(): column = column - jnp.dot(lower, row_of, precision=lax.Precision.HIGHEST)  108 us
    dot_general x128, matrix products, row_step(): jnp.dot(row_of, inverse, precision=lax.Precision.HIGHEST)  107 us
    dot_general x128, matrix products, row_step(): row_of = jnp.dot(picker, lower, precision=lax.Precision.HIGHEST)  105 us
    another operation x1, loops' own time, lower_factor(): return lax.fori_loop(0, order, column_step, jnp.zeros_like(gram))  94 us
    all_gather x1, waiting for transfers between devices, shards(): blocks = lax.all_gather(gram_local, ('gx', 'gy'), axis=0, tiled=False)  57.8 us
    ppermute x10, starting transfers between devices, extended(): lax.ppermute(lax.slice_in_dim(block, block.shape[dim] - width, None, axis...  32.5 us
    div x8, other arithmetic, fourth(): return (segment(0) - segment(4) + 8.0 * (segment(3) - segment(1))) / 12.0  32.5 us
    slice x4, local copies, waits for them, and re-layouts, shards(): sampled = velocities[:, ::2, ::2, ::2]  27.8 us
  transfers between devices with their start and end apart: 22, of which 6 were waited for; matrix products, arithmetic and copies ran while one was open for 8% of the time, Pallas kernels for 0%

profile of v1, /device:TPU:1, one launch (start us, length us, event | category | flops | bytes accessed | tf_op | source)
XLA Modules:
  0.0 814.7 jit_solution(13030031870366113874)
XLA Ops:
  10.5 5.2 collective-permute-start
  18.5 4.9 collective-permute-start.4
  31.3 4.7 collective-permute-start.3
  44.7 4.6 pad_maximum_fusion
  63.1 3.5 fusion.87
  67.4 4.9 fusion.56
  72.4 3.3 add_multiply_fusion.3
  79.5 3.9 collective-permute-start.8
  86.8 5.7 collective-permute-done.9
  92.8 3.6 collective-permute-start.11
  104.1 3.5 fusion.78
  108.5 4.5 fusion.50
  113.0 3.3 add_multiply_fusion.2
  123.0 6.1 collective-permute-start.12
  132.6 6.9 slice.1053
  146.8 3.0 collective-permute-start.15
  152.7 6.9 slice.1055
  165.3 2.9 fusion.74
  168.3 3.5 fusion.69
  172.6 4.9 fusion.44
  177.6 3.3 add_multiply_fusion.1
  191.6 5.8 collective-permute-start.16
  199.1 6.9 slice.1057
  212.1 3.9 collective-permute-start.19
  223.9 3.5 fusion.60
  228.2 4.9 fusion.38
  233.2 3.3 add_multiply_fusion
  241.1 7.0 slice.1059
  250.0 7.7 reduce-scatter.2.cloned.1.call-done
  260.7 57.8 %all-gather.3.cloned.1.call-done = f32[4096,128]{1,0:T(8,128)} async-done(((f32[128,128]{1,0:T(8,128)}), f32[4096,128]{1,0:T(8,128)}) %all-gather.3.cloned.1.call-update) | async-done | bytes 2097168 | tf_op jit(solution)/shard_map/all_gather | solution.py:154
  320.2 255.8 %while.30 = (s32[]{:T(128)}, f32[128,128]{1,0:T(8,128)S(1)}, f32[128,128]{1,0:T(8,128)S(1)}, s32[]{:T(128)}, s32[]{:T(128)}) while((s32[]{:T(128)}, f32[128,128]{1,0:T(8,128)S(1)}, f32[128,128]{1,0:T(8,128)S(1)}, s32[]{:T(128)}, s32[]{:T(128)}) %tuple.121), condition=%wide.region_7.8_spmd.clone.clone, body=%wide.region_5.7_spmd.clone.clone.sunk | while | flops 673410 | bytes 332917 | solution.py:96
  576.7 230.0 %while.29 = (s32[]{:T(128)}, f32[128,128]{1,0:T(8,128)S(1)}, f32[128,128]{1,0:T(8,128)S(1)}, s32[]{:T(128)}, s32[]{:T(128)}) while((s32[]{:T(128)}, f32[128,128]{1,0:T(8,128)S(1)}, f32[128,128]{1,0:T(8,128)S(1)}, s32[]{:T(128)}, s32[]{:T(128)}) %tuple.124), condition=%wide.region_10.11_spmd.clone, body=%wide.region_8.10_spmd.clone.sunk | while | flops 460034 | bytes 265316 | solution.py:110
  (1550 shorter events, 506.7 us)
Async XLA Ops:
  7.2 250.5 %reduce-scatter.2.cloned.1.call-start = ((), (), s32[]{:S(2)}) async-start(), calls=%async_computation.2 | async-start | bytes 147456 | tf_op jit(solution)/shard_map/reduce_scatter | solution.py:143
  9.2 17.0 %collective-permute-start.1 = (f32[5,32,2,128]{3,1,2,0:T(8,128)}, f32[5,32,2,128]{3,1,2,0:T(8,128)}, u32[]{:S(2)}, u32[]{:S(2)}) collective-permute-start(f32[5,32,2,128]{3,1,2,0:T(8,128)} %copy.382), channel_id=1, source_target_pairs={{2,0},{4,2},{6,4},{8,6},{10,8},{12,10},{14,12},{16,14},{18,16},{20... | collective-permute-start | bytes 491528 | tf_op jit(solution)/shard_map/ppermute | solution.py:19
  10.5 14.3 %collective-permute-start = (f32[5,32,2,128]{3,1,2,0:T(8,128)S(1)}, f32[5,32,2,128]{3,1,2,0:T(8,128)}, u32[]{:S(2)}, u32[]{:S(2)}) collective-permute-start(f32[5,32,2,128]{3,1,2,0:T(8,128)S(1)} %copy.381), channel_id=1, source_target_pairs={{0,2},{2,4},{4,6},{6,8},{8,10},{10,12},{12,14},{14,16},{16,18},{18... | collective-permute-start | bytes 491528 | tf_op jit(solution)/shard_map/ppermute | solution.py:16
  16.5 34.9 %collective-permute-start.5 = (f32[3,32,4,128]{3,1,2,0:T(8,128)}, f32[3,32,4,128]{3,1,2,0:T(8,128)}, u32[]{:S(2)}, u32[]{:S(2)}) collective-permute-start(f32[3,32,4,128]{3,1,2,0:T(8,128)} %copy.384), channel_id=1, source_target_pairs={{2,0},{4,2},{6,4},{8,6},{10,8},{12,10},{14,12},{16,14},{18,16},{20... | collective-permute-start | bytes 589832 | tf_op jit(solution)/shard_map/ppermute | solution.py:19
  18.5 30.8 %collective-permute-start.4 = (f32[3,32,4,128]{3,1,2,0:T(8,128)}, f32[3,32,4,128]{3,1,2,0:T(8,128)}, u32[]{:S(2)}, u32[]{:S(2)}) collective-permute-start(f32[3,32,4,128]{3,1,2,0:T(8,128)} %copy.383), channel_id=1, source_target_pairs={{0,2},{2,4},{4,6},{6,8},{8,10},{10,12},{12,14},{14,16},{16,18},{18... | collective-permute-start | bytes 589832 | tf_op jit(solution)/shard_map/ppermute | solution.py:16
  26.2 10.5 %copy-start.50 = (f32[5,32,2,128]{1,3,2,0:T(8,128)}, f32[5,32,2,128]{1,3,2,0:T(8,128)S(1)}, u32[]{:S(2)}) copy-start(f32[5,32,2,128]{1,3,2,0:T(8,128)S(1)} %copy.315) | copy-start | bytes 491524
  30.0 14.7 %collective-permute-start.2 = (f32[5,32,12,2]{1,3,2,0:T(2,128)}, f32[5,32,12,2]{1,3,2,0:T(2,128)}, u32[]{:S(2)}, u32[]{:S(2)}) collective-permute-start(f32[5,32,12,2]{1,3,2,0:T(2,128)} %get-tuple-element.285), channel_id=1, source_target_pairs={{0,1},{2,3},{4,5},{6,7},{8,9},{10,11},{12,13},{14,15},{16,17},{18,... | collective-permute-start | bytes 46088 | tf_op jit(solution)/shard_map/ppermute | solution.py:16
  31.3 13.4 %collective-permute-start.3 = (f32[5,32,12,2]{1,3,2,0:T(2,128)}, f32[5,32,12,2]{1,3,2,0:T(2,128)}, u32[]{:S(2)}, u32[]{:S(2)}) collective-permute-start(f32[5,32,12,2]{1,3,2,0:T(2,128)} %get-tuple-element.286), channel_id=1, source_target_pairs={{1,0},{3,2},{5,4},{7,6},{9,8},{11,10},{13,12},{15,14},{17,16},{19,... | collective-permute-start | bytes 46088 | tf_op jit(solution)/shard_map/ppermute | solution.py:19
  37.8 37.8 %copy-start.25 = (f32[32,8,128]{0,2,1:T(8,128)}, f32[32,8,128]{0,2,1:T(8,128)S(1)}, u32[]{:S(2)}) copy-start(f32[32,8,128]{0,2,1:T(8,128)S(1)} %copy.331) | copy-start | bytes 393220
  39.5 37.1 %copy-start.6 = (f32[3,32,8,128]{1,3,2,0:T(8,128)}, f32[3,32,8,128]{1,3,2,0:T(8,128)S(1)}, u32[]{:S(2)}) copy-start(f32[3,32,8,128]{1,3,2,0:T(8,128)S(1)} %copy.309) | copy-start | bytes 1179652
  39.7 35.9 %copy-start.29 = (f32[1,32,8,128]{1,3,2,0:T(8,128)}, f32[1,32,8,128]{1,3,2,0:T(8,128)S(1)}, u32[]{:S(2)}) copy-start(f32[1,32,8,128]{1,3,2,0:T(8,128)S(1)} %copy.385) | copy-start | bytes 393220
  40.0 35.7 %copy-start.33 = (f32[1,32,8,128]{1,3,2,0:T(8,128)}, f32[1,32,8,128]{1,3,2,0:T(8,128)S(1)}, u32[]{:S(2)}) copy-start(f32[1,32,8,128]{1,3,2,0:T(8,128)S(1)} %copy.386) | copy-start | bytes 393220
  54.5 4.8 collective-permute-start.7
  55.9 3.4 collective-permute-start.6
  79.5 7.0 collective-permute-start.8
  83.6 8.8 %collective-permute-start.9 = (f32[3,32,4,128]{3,1,2,0:T(8,128)S(1)}, f32[3,32,4,128]{3,1,2,0:T(8,128)S(1)}, u32[]{:S(2)}, u32[]{:S(2)}) collective-permute-start(f32[3,32,4,128]{3,1,2,0:T(8,128)S(1)} %copy.336), channel_id=1, source_target_pairs={{2,0},{4,2},{6,4},{8,6},{10,8},{12,10},{14,12},{16,14},{18,16},{20... | collective-permute-start | bytes 589832 | tf_op jit(solution)/shard_map/ppermute | solution.py:19
  92.8 4.9 collective-permute-start.11
  96.4 3.2 collective-permute-start.10
  123.0 17.4 %collective-permute-start.12 = (f32[3,32,4,128]{3,1,2,0:T(8,128)}, f32[3,32,4,128]{3,1,2,0:T(8,128)}, u32[]{:S(2)}, u32[]{:S(2)}) collective-permute-start(f32[3,32,4,128]{3,1,2,0:T(8,128)} %copy.348), channel_id=1, source_target_pairs={{0,2},{2,4},{4,6},{6,8},{8,10},{10,12},{12,14},{14,16},{16,18},{18... | collective-permute-start | bytes 589832 | tf_op jit(solution)/shard_map/ppermute | solution.py:16
  131.1 11.3 %collective-permute-start.13 = (f32[3,32,4,128]{3,1,2,0:T(8,128)}, f32[3,32,4,128]{3,1,2,0:T(8,128)}, u32[]{:S(2)}, u32[]{:S(2)}) collective-permute-start(f32[3,32,4,128]{3,1,2,0:T(8,128)} %copy.349), channel_id=1, source_target_pairs={{2,0},{4,2},{6,4},{8,6},{10,8},{12,10},{14,12},{16,14},{18,16},{20... | collective-permute-start | bytes 589832 | tf_op jit(solution)/shard_map/ppermute | solution.py:19
  146.8 13.6 %collective-permute-start.15 = (f32[3,32,16,4]{1,2,3,0:T(8,128)}, f32[3,32,16,4]{1,2,3,0:T(8,128)}, u32[]{:S(2)}, u32[]{:S(2)}) collective-permute-start(f32[3,32,16,4]{1,2,3,0:T(8,128)} %copy.353), channel_id=1, source_target_pairs={{1,0},{3,2},{5,4},{7,6},{9,8},{11,10},{13,12},{15,14},{17,16},{19,... | collective-permute-start | bytes 73736 | tf_op jit(solution)/shard_map/ppermute | solution.py:19
  149.8 11.6 %collective-permute-start.14 = (f32[3,32,16,4]{1,2,3,0:T(8,128)}, f32[3,32,16,4]{1,2,3,0:T(8,128)}, u32[]{:S(2)}, u32[]{:S(2)}) collective-permute-start(f32[3,32,16,4]{1,2,3,0:T(8,128)} %copy.352), channel_id=1, source_target_pairs={{0,1},{2,3},{4,5},{6,7},{8,9},{10,11},{12,13},{14,15},{16,17},{18,... | collective-permute-start | bytes 73736 | tf_op jit(solution)/shard_map/ppermute | solution.py:16
  186.2 11.2 %copy-start.56 = (f32[4,48,128]{2,1,0:T(8,128)S(1)}, f32[4,48,128]{2,1,0:T(8,128)}, u32[]{:S(2)}) copy-start(f32[4,48,128]{2,1,0:T(8,128)} %fusion.203) | copy-start | bytes 294916
  186.2 11.2 %copy-start.59 = (f32[4,3,16,64]{3,2,1,0:T(8,128)S(1)}, f32[4,3,16,64]{3,2,1,0:T(8,128)}, u32[]{:S(2)}) copy-start(f32[4,3,16,64]{3,2,1,0:T(8,128)} %copy.376) | copy-start | bytes 147460
  188.2 22.9 %copy-start.5 = (f32[3,32,8,128]{1,3,2,0:T(8,128)S(1)}, f32[3,32,8,128]{1,3,2,0:T(8,128)}, u32[]{:S(2)}) copy-start(f32[3,32,8,128]{1,3,2,0:T(8,128)} %copy-done.4) | copy-start | bytes 1179652
  190.3 18.6 %collective-permute-start.17 = (f32[3,32,4,128]{3,1,2,0:T(8,128)}, f32[3,32,4,128]{3,1,2,0:T(8,128)}, u32[]{:S(2)}, u32[]{:S(2)}) collective-permute-start(f32[3,32,4,128]{3,1,2,0:T(8,128)} %copy.362), channel_id=1, source_target_pairs={{2,0},{4,2},{6,4},{8,6},{10,8},{12,10},{14,12},{16,14},{18,16},{20... | collective-permute-start | bytes 589832 | tf_op jit(solution)/shard_map/ppermute | solution.py:19
  191.6 15.2 %collective-permute-start.16 = (f32[3,32,4,128]{3,1,2,0:T(8,128)}, f32[3,32,4,128]{3,1,2,0:T(8,128)}, u32[]{:S(2)}, u32[]{:S(2)}) collective-permute-start(f32[3,32,4,128]{3,1,2,0:T(8,128)} %copy.361), channel_id=1, source_target_pairs={{0,2},{2,4},{4,6},{6,8},{8,10},{10,12},{12,14},{14,16},{16,18},{18... | collective-permute-start | bytes 589832 | tf_op jit(solution)/shard_map/ppermute | solution.py:16
  212.1 6.3 collective-permute-start.19
  216.1 3.2 collective-permute-start.18
  241.1 18.4 %copy-start.49 = (f32[3,32,8,128]{1,3,2,0:T(8,128)S(1)}, f32[3,32,8,128]{1,3,2,0:T(8,128)}, u32[]{:S(2)}) copy-start(f32[3,32,8,128]{1,3,2,0:T(8,128)} %get-tuple-element.231) | copy-start | bytes 1179652
  249.9 68.5 %all-gather.3.cloned.1.call-start = ((), (), s32[]{:S(2)}) async-start(), calls=%async_computation.1 | async-start | bytes 2162688 | tf_op jit(solution)/shard_map/all_gather | solution.py:154
  318.5 488.3 %copy-start.55 = (f32[4,24,128]{2,1,0:T(8,128)S(1)}, f32[4,24,128]{2,1,0:T(8,128)}, u32[]{:S(2)}) copy-start(f32[4,24,128]{2,1,0:T(8,128)} %reduce-scatter.2.cloned.1.call-done) | copy-start | bytes 147460
  (51 other events, 188.8 us)
Sparse Core Ops, SparseCore 0:
  250.0 7.5 reduce-scatter.1
  261.1 57.3 all-gather.2
